TPU v7x, 128 devices: a whole 4x4x4 slice. The times are simulated.
128 devices in a mesh: tok: 16 (over x, y), head: 8 (over z, core).
Axes of the slice: x: 4, y: 4, z: 4, core: 2. Of those that a mesh axis runs over, the one named last changes fastest.
Arguments:
- hidden: float32 [8192, 5376], P('tok', 'head'), may hold values from -8 to 8
- queries: float32 [8192, 2048], P('tok', 'head'), may hold values from -4000 to 4000
- out_grad: float32 [8192, 2048], P('tok', 'head'), may hold values from -6 to 6
- w_key: float32 [5376, 1024], P('head', 'tok'), may hold values from -1 to 1
- w_value: float32 [5376, 1024], P('head', 'tok'), may hold values from -0.078125 to 0.078125
- fork_tile: int32 [15], replicated, may hold values from 0 to 57, as said below
- live_len: int32 [16], replicated, may hold values from 257 to 512, as said below
Outputs:
- grad_query: float32 [8192, 2048], P('tok', 'head')
- grad_key: float32 [8192, 1024], P('tok', 'head')
- grad_value: float32 [8192, 1024], P('tok', 'head')
- grad_w_key: float32 [5376, 1024], P('head', 'tok')
- grad_w_value: float32 [5376, 1024], P('head', 'tok')
Inputs may be any that keep to these rules, and one draw needn't show every extreme that they name: fork_tile[b - 1] lies in branch b - 1 or b - 2 (branch 0 counts), among that branch's first 2 tiles, and those tiles are live. `live_len`: branch 0 is fully live.
All inputs are finite; a program needn't handle non-finite values.
Results may differ from a plain program's by a relative error of at most 0.0005.
Values sent between devices are 32-bit elements; how exact they have to be, the bound alone decides.
A program may use at most 128 MiB of HBM per device.

v0:
```python
import jax
import jax.numpy as jnp
from jax import lax
from jax.sharding import Mesh
from jax.sharding import PartitionSpec as P

HEAD_DIM = 128
TILE = 128
CAP = 2
TOK_DEV = 512
TOK = ("tok_0", "tok_1")


logit_scale = 168.0 ** (-0.5)
highest = lax.Precision.HIGHEST


def in_blocks(shard, dim, count):
    before, after = (shard.shape[:dim], shard.shape[dim + 1 :])
    return jnp.moveaxis(shard.reshape(*before, count, -1, *after), dim, 0)


def summed_on_arrival(shard, axis, dim):
    blocks = in_blocks(shard, dim, lax.axis_size(axis))
    arrived = lax.all_to_all(blocks, axis, split_axis=0, concat_axis=0, tiled=True)
    return arrived.sum(axis=0)


def summed_rows(running, axes):
    for axis in axes:
        running = lax.psum_scatter(running, axis, scatter_dimension=0, tiled=True)
    return running


def path_table(fork_tile, owners, tile_count):
    initial = jnp.full((owners, owners), -1, jnp.int32)

    def visit_branch(branch, path_rows):
        fork_at = fork_tile[branch - 1]
        parent = fork_at // tile_count
        inherited = path_rows[parent].at[parent].set(fork_at % tile_count)
        return path_rows.at[branch].set(inherited)

    return lax.fori_loop(1, owners, visit_branch, initial)


def visible_mask(entries_row, live_count, row_count, owners):
    slot_index = jnp.arange(owners * CAP * TILE)
    owner_of = slot_index // (CAP * TILE)
    tile_of = slot_index % (CAP * TILE) // TILE
    remote = (tile_of <= entries_row[owner_of])[None, :]
    positions = jnp.arange(row_count)
    local_part = (positions[None, :] <= positions[:, None]) & (positions[None, :] < live_count)
    return jnp.concatenate(
        [jnp.broadcast_to(remote, (row_count, remote.shape[1])), local_part], axis=1
    )


def attend(query_rows, grad_rows, key_rows, value_rows, visible):
    query_heads = query_rows.shape[1] // HEAD_DIM
    kv_heads = key_rows.shape[1] // HEAD_DIM
    group_size = query_heads // kv_heads
    query_grads = []
    key_grads = [jnp.zeros((key_rows.shape[0], HEAD_DIM), jnp.float32)]
    value_grads = [jnp.zeros((key_rows.shape[0], HEAD_DIM), jnp.float32)]
    for head_index in range(query_heads):
        kv_index = head_index // group_size
        query_head = query_rows[:, head_index * HEAD_DIM : (head_index + 1) * HEAD_DIM]
        grad_head = grad_rows[:, head_index * HEAD_DIM : (head_index + 1) * HEAD_DIM]
        scores = jnp.dot(query_head, key_rows.T, precision=highest) * logit_scale
        scores = jnp.where(visible, scores, -1e30)
        largest = jnp.max(scores, axis=1, keepdims=True)
        weights = jnp.where(visible, jnp.exp(scores - largest), 0.0)
        weights = weights / jnp.sum(weights, axis=1, keepdims=True)
        output = jnp.dot(weights, value_rows, precision=highest)
        delta_row = jnp.sum(grad_head * output, axis=1, keepdims=True)
        grad_prob = jnp.dot(grad_head, value_rows.T, precision=highest)
        grad_score = weights * (grad_prob - delta_row)
        query_grads.append(jnp.dot(grad_score, key_rows, precision=highest) * logit_scale)
        key_grads[kv_index] = (
            key_grads[kv_index] + jnp.dot(grad_score.T, query_head, precision=highest) * logit_scale
        )
        value_grads[kv_index] = value_grads[kv_index] + jnp.dot(
            weights.T, grad_head, precision=highest
        )
    return (jnp.concatenate(query_grads, axis=1), key_grads[0], value_grads[0])


def shards(hidden, queries, out_grad, w_key, w_value, fork_tile, live_len):
    owners = lax.axis_size(TOK)
    branch = lax.axis_index(TOK)
    stacked = jnp.stack([w_key, w_value])
    partials = jnp.einsum(
        "td,sdc->stc", hidden, lax.all_gather(stacked, TOK, axis=2, tiled=True), precision=highest
    )
    projected = lax.psum_scatter(partials, "head", scatter_dimension=2, tiled=True)
    fork_span = CAP * TILE
    remote_count = owners * fork_span
    fork_rows = lax.all_gather(projected[:, :fork_span], TOK, axis=1, tiled=True)
    path_rows = path_table(fork_tile, owners, TOK_DEV // TILE)
    visible = visible_mask(path_rows[branch], live_len[branch], TOK_DEV, owners)
    live_rows = (jnp.arange(TOK_DEV) < live_len[branch]).astype(jnp.float32)[:, None]
    key_rows = jnp.concatenate([fork_rows[0], projected[0]], axis=0)
    value_rows = jnp.concatenate([fork_rows[1], projected[1]], axis=0)
    grad_query, grad_keys, grad_values = attend(
        queries, out_grad * live_rows, key_rows, value_rows, visible
    )
    remote = jnp.stack([grad_keys[:remote_count], grad_values[:remote_count]])
    returned = summed_on_arrival(remote, TOK, 1)
    own_grads = jnp.stack([grad_keys[remote_count:], grad_values[remote_count:]])
    own_grads = own_grads.at[:, :fork_span].add(returned)
    every_column = lax.all_gather(own_grads, "head", axis=2, tiled=True)
    summed = summed_rows(jnp.einsum("stc,td->csd", every_column, hidden, precision=highest), TOK)
    grad_w_key = summed[:, 0, :].T
    grad_w_value = summed[:, 1, :].T
    return (grad_query, own_grads[0], own_grads[1], grad_w_key, grad_w_value)


def solution(mesh):
    torus = Mesh(mesh.devices.reshape(4, 4, mesh.shape["head"]), ("tok_0", "tok_1", "head"))
    in_specs = (
        P(TOK, "head"),
        P(TOK, "head"),
        P(TOK, "head"),
        P("head", TOK),
        P("head", TOK),
        P(),
        P(),
    )
    out_specs = (P(TOK, "head"), P(TOK, "head"), P(TOK, "head"), P("head", TOK), P("head", TOK))
    return jax.shard_map(
        shards, mesh=torus, in_specs=in_specs, out_specs=out_specs, check_vma=False
    )
```

profile of v0, /device:TPU:0, one launch (start us, length us, event | category | flops | bytes accessed | tf_op | source)
XLA Modules:
  0.0 594.1 jit_solution(3947672930276642152)
XLA Ops:
  7.2 1.9 pad_maximum_fusion.12
  9.2 65.2 %all-gather.4.cloned.1.call-done = f32[2,672,1024]{1,2,0:T(8,128)} async-done(((f32[2,672,64]{1,2,0:T(8,128)}), f32[2,672,1024]{1,2,0:T(8,128)}) %all-gather.4.cloned.1.call-update) | async-done | bytes 5505040 | tf_op jit(solution)/shard_map/all_gather | solution.py:94
  74.4 13.4 %convolution_bitcast_fusion.1 = f32[2,512,1024]{1,2,0:T(8,128)} fusion(f32[2,672,1024]{1,2,0:T(8,128)} %all-gather.4.cloned.1.call-done, f32[512,672]{0,1:T(8,128)S(1)} %copy-done), kind=kOutput, calls=%fused_computation.21 | convolution fusion | flops 8455716864 | bytes 11075584 | tf_op jit(solution)/shard_map/td,sdc->stc/dot_general | solution.py:93
  87.8 0.9 copy-done.14
  90.1 35.6 %reduce-scatter.3.cloned.1.call-done = f32[2,512,128]{1,2,0:T(8,128)} async-done(((f32[2,512,1024]{1,2,0:T(8,128)}), f32[2,512,128]{1,2,0:T(8,128)}) %reduce-scatter.3.cloned.1.call-update) | async-done | bytes 524304 | tf_op jit(solution)/shard_map/reduce_scatter | solution.py:96
  125.7 1.7 slice.170
  127.5 90.7 %while.22 = (s32[]{:T(128)}, s32[16,16]{1,0:T(8,128)S(1)}, s32[15]{0:T(128)S(1)}, s32[]{:T(128)}, s32[]{:T(128)}, /*index=5*/s32[]{:T(128)}, s32[]{:T(128)}, s32...) while((s32[]{:T(128)}, s32[16,16]{1,0:T(8,128)S(1)}, ...), condition=%wide.region_2.3_spmd, body=%wide.region_0.2_spmd.sunk | while | flops 57 | bytes 960 | solution.py:44
  132.0 0.7 and_reduce_fusion.2
  137.9 0.7 and_reduce_fusion.2
  144.0 0.7 and_reduce_fusion.2
  150.0 0.7 and_reduce_fusion.2
  156.1 0.7 and_reduce_fusion.2
  204.4 0.7 and_reduce_fusion.2
  218.2 0.7 fusion.43
  219.0 4.3 compare_select_fusion.1
  223.2 5.8 fusion.24
  229.9 1.1 slice_bitcast_fusion.7
  231.0 2.7 slice_bitcast_fusion.1
  233.7 10.5 %fusion.45 = (f32[512]{0:T(512)S(1)}, f32[512,4608]{0,1:T(8,128)S(1)}) fusion(f32[512,256]{1,0:T(8,128)S(1)} %copy-done.13, f32[512,128]{0,1:T(8,128)S(1)} %get-tuple-element.272, f32[4096,128]{0,1:T(8,128)S(1)} %get-tuple-element.266, pred[512,512]{0,1:T(32,128)(4,1)S(1)} %fusion.9, pred[4608]{0:T(1024)(128)(4,1)S(1)} %pad.24.clone), kind=kOutput, calls=%fused_computation.110 | convolution fusion | flops 3633905152 | bytes 12327936 | tf_op jit(solution)/shard_map/dot_general | solution.py:70
  244.2 10.9 %fusion.44 = (f32[512]{0:T(512)S(1)}, f32[512,4608]{0,1:T(8,128)S(1)}) fusion(f32[512,256]{1,0:T(8,128)S(1)} %copy-done.13, f32[512,128]{0,1:T(8,128)S(1)} %get-tuple-element.272, f32[4096,128]{0,1:T(8,128)S(1)} %get-tuple-element.266, pred[512,512]{0,1:T(32,128)(4,1)S(1)} %fusion.9, pred[4608]{0:T(1024)(128)(4,1)S(1)} %pad.24.clone), kind=kOutput, calls=%fused_computation.109 | convolution fusion | flops 3633905152 | bytes 12327936 | tf_op jit(solution)/shard_map/dot_general | solution.py:70
  255.1 6.1 %fusion.1 = (f32[512]{0:T(512)S(1)}, f32[512]{0:T(512)S(1)}) fusion(f32[512,4608]{0,1:T(8,128)S(1)} %get-tuple-element.291, pred[512,512]{0,1:T(32,128)(4,1)S(1)} %fusion.9, f32[512]{0:T(512)S(1)} %get-tuple-element.290, pred[4608]{0:T(1024)(128)(4,1)S(1)} %pad.24.clone, f32[512,4608]{0,1:T(8,128)S(1)} %get-tuple-element.293, f32[512]{0:T(512)S(1)} %get-tuple-element.292), kind=kLoop, calls=%fused_computation.11 | loop fusion | flops 16514048 | bytes 19149312 | tf_op jit(solution)/shard_map/reduce_sum | solution.py:74
  261.2 11.9 %fusion.20 = f32[4608,128]{1,0:T(8,128)} fusion(f32[512,256]{0,1:T(8,128)S(1)} %broadcast_multiply_fusion, f32[512,4608]{0,1:T(8,128)S(1)} %get-tuple-element.291, pred[512,512]{0,1:T(32,128)(4,1)S(1)} %fusion.9, f32[512]{0:T(512)S(1)} %get-tuple-element.258, f32[512]{0:T(512)S(1)} %get-tuple-element.290, pred[4608]{0:T(1024)(128)(4,1)S(1)} %pad.24.clone), kind=kOutput, calls=%fused_computation.56 | convolution fusion | flops 3633315840 | bytes 12329984 | tf_op jit(solution)/shard_map/dot_general | solution.py:83
  273.1 7.2 %fusion.7 = f32[512]{0:T(512)S(1)} fusion(f32[512,128]{0,1:T(8,128)S(1)} %get-tuple-element.273, f32[4096,128]{0,1:T(8,128)S(1)} %get-tuple-element.267, f32[512,256]{0,1:T(8,128)S(1)} %broadcast_multiply_fusion, f32[512,4608]{0,1:T(8,128)S(1)} %get-tuple-element.291, pred[512,512]{0,1:T(32,128)(4,1)S(1)} %fusion.9, f32[512]{0:T(512)S(1)} %get-tuple-element.258, ...), kind=kOutput, calls=%fused_computation.30 | convolution fusion | flops 3634036224 | bytes 12331520 | tf_op jit(solution)/shard_map/dot_general | solution.py:75
  280.3 7.4 %fusion.8 = f32[512]{0:T(512)S(1)} fusion(f32[512,128]{0,1:T(8,128)S(1)} %get-tuple-element.273, f32[4096,128]{0,1:T(8,128)S(1)} %get-tuple-element.267, f32[512,256]{0,1:T(8,128)S(1)} %broadcast_multiply_fusion, f32[512,4608]{0,1:T(8,128)S(1)} %get-tuple-element.293, pred[512,512]{0,1:T(32,128)(4,1)S(1)} %fusion.9, f32[512]{0:T(512)S(1)} %get-tuple-element.259, ...), kind=kOutput, calls=%fused_computation.31 | convolution fusion | flops 3634036224 | bytes 12331520 | tf_op jit(solution)/shard_map/dot_general | solution.py:75
  287.7 13.4 %subtract_multiply_fusion.1 = f32[512,4608]{0,1:T(8,128)S(1)} fusion(f32[512]{0:T(512)S(1)} %fusion.7, f32[512,128]{0,1:T(8,128)S(1)} %get-tuple-element.273, f32[4096,128]{0,1:T(8,128)S(1)} %get-tuple-element.267, f32[512,256]{0,1:T(8,128)S(1)} %broadcast_multiply_fusion, f32[512]{0:T(512)S(1)} %get-tuple-element.258, f32[512,4608]{0,1:T(8,128)} %copy-done.7, ...), kind=kOutput, calls=%fused_computation.7 | convolution fusion | flops 3638624256 | bytes 21769216 | tf_op jit(solution)/shard_map/dot_general | solution.py:77
  301.2 12.5 %convolution_add_fusion = f32[4608,128]{1,0:T(8,128)S(1)} fusion(f32[4608,128]{1,0:T(8,128)} %fusion.20, f32[512,256]{0,1:T(8,128)S(1)} %broadcast_multiply_fusion, f32[512,4608]{0,1:T(8,128)S(1)} %get-tuple-element.293, pred[512,512]{0,1:T(32,128)(4,1)S(1)} %fusion.9, f32[512]{0:T(512)S(1)} %get-tuple-element.259, f32[512]{0:T(512)S(1)} %get-tuple-element.292, ...), kind=kOutput, calls=%fused_computation.14 | convolution fusion | flops 3633905664 | bytes 14689280 | tf_op jit(solution)/shard_map/dot_general | solution.py:83
  313.7 14.6 %subtract_multiply_fusion = f32[512,4608]{0,1:T(8,128)S(1)} fusion(f32[512]{0:T(512)S(1)} %fusion.8, f32[512,128]{0,1:T(8,128)S(1)} %get-tuple-element.273, f32[4096,128]{0,1:T(8,128)S(1)} %get-tuple-element.267, f32[512,256]{0,1:T(8,128)S(1)} %broadcast_multiply_fusion, f32[512]{0:T(512)S(1)} %get-tuple-element.259, f32[512,4608]{0,1:T(8,128)} %copy-done.6, ...), kind=kOutput, calls=%fused_computation.5 | convolution fusion | flops 3638624256 | bytes 21769216 | tf_op jit(solution)/shard_map/dot_general | solution.py:77
  328.4 7.9 %fusion.15 = f32[4608,128]{1,0:T(8,128)S(1)} fusion(f32[512,4608]{0,1:T(8,128)S(1)} %subtract_multiply_fusion.1, f32[512,256]{1,0:T(8,128)S(1)} %copy-done.13), kind=kOutput, calls=%fused_computation.51 | convolution fusion | flops 3623878656 | bytes 12058624 | tf_op jit(solution)/shard_map/dot_general | solution.py:81
  336.3 8.1 %fusion.4 = f32[4608,128]{1,0:T(8,128)S(1)} fusion(f32[4608,128]{1,0:T(8,128)S(1)} %fusion.15, f32[512,4608]{0,1:T(8,128)S(1)} %subtract_multiply_fusion, f32[512,256]{1,0:T(8,128)S(1)} %copy-done.13), kind=kOutput, calls=%fused_computation.16 | convolution fusion | flops 3625058304 | bytes 14417920 | tf_op jit(solution)/shard_map/dot_general | solution.py:81
  344.4 1.4 copy-done.3
  345.9 1.4 slice-done.3
  347.4 2.3 maximum_bitcast_fusion
  349.7 6.9 %all-to-all-start = ((f32[16,2,256,128]{3,2,1,0:T(8,128)}), f32[16,2,256,128]{3,2,1,0:T(8,128)}, u32[]{:S(2)}, u32[]{:S(2)}) async-start(f32[16,2,256,128]{3,2,1,0:T(8,128)} %maximum_bitcast_fusion), calls=%async_computation.1 | async-start | bytes 8388608 | tf_op jit(solution)/shard_map/all_to_all | solution.py:25
  356.6 1.0 slice_bitcast_fusion.4
  357.6 1.0 slice_bitcast_fusion.5
  358.6 49.5 %all-to-all-done = f32[16,2,256,128]{3,2,1,0:T(8,128)} async-done(((f32[16,2,256,128]{3,2,1,0:T(8,128)}), f32[16,2,256,128]{3,2,1,0:T(8,128)}, u32[]{:S(2)}, u32[]{:S(2)}) %all-to-all-start) | async-done | bytes 4194336 | tf_op jit(solution)/shard_map/all_to_all | solution.py:25
  408.1 2.4 reduce_sum.49
  410.6 0.8 copy-done.9
  411.4 47.8 %all-gather.8.cloned.1.call-done = f32[2,512,1024]{2,1,0:T(8,128)} async-done(((f32[2,512,128]{2,1,0:T(8,128)}), f32[2,512,1024]{2,1,0:T(8,128)}) %all-gather.8.cloned.1.call-update) | async-done | bytes 4194320 | tf_op jit(solution)/shard_map/all_gather | solution.py:112
  459.3 12.4 %convolution_bitcast_fusion = f32[1024,2,672]{0,2,1:T(8,128)} fusion(f32[2,512,1024]{2,1,0:T(8,128)} %all-gather.8.cloned.1.call-done, f32[512,672]{0,1:T(8,128)S(1)} %copy-done), kind=kOutput, calls=%fused_computation.18 | convolution fusion | flops 8455716864 | bytes 11075584 | tf_op jit(solution)/shard_map/stc,td->csd/dot_general | solution.py:113
  471.7 58.4 %reduce-scatter.5.cloned.1.call-done = f32[256,2,672]{0,2,1:T(8,128)} async-done(((f32[1024,2,672]{0,2,1:T(8,128)}), f32[256,2,672]{0,2,1:T(8,128)}) %reduce-scatter.5.cloned.1.call-update) | async-done | bytes 1376272 | tf_op jit(solution)/shard_map/reduce_scatter | solution.py:31
  530.1 3.7 copy.29
  535.1 9.0 %convolution_multiply_fusion = f32[512,128]{0,1:T(8,128)S(1)} fusion(f32[512,4608]{0,1:T(8,128)} %copy-done.1, f32[512,128]{0,1:T(8,128)S(1)} %copy-done.12, f32[4096,128]{0,1:T(8,128)} %copy-done.4), kind=kOutput, calls=%fused_computation.26 | convolution fusion | flops 3624534016 | bytes 12058624 | tf_op jit(solution)/shard_map/dot_general | solution.py:79
  544.2 5.4 convolution_multiply_fusion.2
  549.6 1.0 copy.30
  550.6 0.8 slice_bitcast_fusion.2
  551.5 32.7 %all-reduce.3.cloned.1.call-done = f32[256,2,672]{2,1,0:T(2,128)} async-done(((f32[256,2,672]{2,1,0:T(2,128)}), f32[256,2,672]{2,1,0:T(2,128)}) %all-reduce.3.cloned.1.call-update) | async-done | bytes 1376272
  584.1 1.5 constant_dynamic-slice_fusion.2
  (179 shorter events, 41.8 us)
Async XLA Ops:
  7.2 67.2 %copy-start = (f32[512,672]{0,1:T(8,128)S(1)}, f32[512,672]{0,1:T(8,128)}, u32[]{:S(2)}) copy-start(f32[512,672]{0,1:T(8,128)} %param.15) | copy-start | bytes 4128772
  7.2 67.2 %all-gather.4.cloned.1.call-start = ((), (), s32[]{:S(2)}) async-start(), calls=%async_computation.3 | async-start | bytes 6684672 | tf_op jit(solution)/shard_map/all_gather | solution.py:94
  9.1 116.6 %reduce-scatter.3.cloned.1.call-start = ((), (), s32[]{:S(2)}) async-start(), calls=%async_computation.4 | async-start | bytes 4718592 | tf_op jit(solution)/shard_map/reduce_scatter | solution.py:96
  87.7 1.0 copy-start.14
  87.7 1.2 copy-start.16
  87.7 39.7 %copy-start.15 = (s32[2]{0:T(128)S(1)}, s32[2]{0:T(128)}, u32[]{:S(2)}) copy-start(s32[2]{0:T(128)} %constant.377.clone.1) | copy-start | bytes 28
  87.7 39.7 %copy-start.17 = (s32[15]{0:T(128)S(1)}, s32[15]{0:T(128)}, u32[]{:S(2)}) copy-start(s32[15]{0:T(128)} %param.20) | copy-start | bytes 184
  87.8 143.2 %all-gather.6.cloned.1.call-start = ((), (), s32[]{:S(2)}) async-start(), calls=%async_computation.5 | async-start | bytes 4456448 | tf_op jit(solution)/shard_map/all_gather | solution.py:99
  230.9 13.2 %copy-start.11 = (f32[512,128]{0,1:T(8,128)}, f32[512,128]{0,1:T(8,128)S(1)}, u32[]{:S(2)}) copy-start(f32[512,128]{0,1:T(8,128)S(1)} %get-tuple-element.272) | copy-start | bytes 786436
  231.0 2.8 copy-start.13
  233.7 10.5 %copy-start.4 = (f32[4096,128]{0,1:T(8,128)}, f32[4096,128]{0,1:T(8,128)S(1)}, u32[]{:S(2)}) copy-start(f32[4096,128]{0,1:T(8,128)S(1)} %get-tuple-element.266) | copy-start | bytes 6291460
  244.2 57.0 %copy-start.6 = (f32[512,4608]{0,1:T(8,128)}, f32[512,4608]{0,1:T(8,128)S(1)}, u32[]{:S(2)}) copy-start(f32[512,4608]{0,1:T(8,128)S(1)} %get-tuple-element.293) | copy-start | bytes 28311556
  255.1 18.0 %copy-start.7 = (f32[512,4608]{0,1:T(8,128)}, f32[512,4608]{0,1:T(8,128)S(1)}, u32[]{:S(2)}) copy-start(f32[512,4608]{0,1:T(8,128)S(1)} %get-tuple-element.291) | copy-start | bytes 28311556
  301.2 27.2 %copy-start.2 = (f32[512,4608]{0,1:T(8,128)}, f32[512,4608]{0,1:T(8,128)S(1)}, u32[]{:S(2)}) copy-start(f32[512,4608]{0,1:T(8,128)S(1)} %subtract_multiply_fusion.1) | copy-start | bytes 28311556
  313.7 14.7 %copy-start.8 = (f32[4608,128]{1,0:T(8,128)}, f32[4608,128]{1,0:T(8,128)S(1)}, u32[]{:S(2)}) copy-start(f32[4608,128]{1,0:T(8,128)S(1)} %convolution_add_fusion) | copy-start | bytes 7077892
  328.4 7.9 %copy-start.1 = (f32[512,4608]{0,1:T(8,128)}, f32[512,4608]{0,1:T(8,128)S(1)}, u32[]{:S(2)}) copy-start(f32[512,4608]{0,1:T(8,128)S(1)} %subtract_multiply_fusion) | copy-start | bytes 28311556
  344.4 1.4 copy-start.3
  345.8 1.6 slice-start.3
  349.7 58.4 %all-to-all-start = ((f32[16,2,256,128]{3,2,1,0:T(8,128)}), f32[16,2,256,128]{3,2,1,0:T(8,128)}, u32[]{:S(2)}, u32[]{:S(2)}) async-start(f32[16,2,256,128]{3,2,1,0:T(8,128)} %maximum_bitcast_fusion), calls=%async_computation.1 | async-start | bytes 8388608 | tf_op jit(solution)/shard_map/all_to_all | solution.py:25
  356.6 102.7 %all-gather.8.cloned.1.call-start = ((), (), s32[]{:S(2)}) async-start(), calls=%async_computation.6 | async-start | bytes 4718592 | tf_op jit(solution)/shard_map/all_gather | solution.py:112
  410.6 0.8 copy-start.9
  411.4 118.7 %reduce-scatter.5.cloned.1.call-start = ((), (), s32[]{:S(2)}) async-start(), calls=%async_computation.7 | async-start | bytes 6881280 | tf_op jit(solution)/shard_map/reduce_scatter | solution.py:31
  471.6 62.2 %copy-start.18 = (u32[128]{0:T(128)S(1)}, u32[128]{0:T(128)}, u32[]{:S(2)}) copy-start(u32[128]{0:T(128)} %constant.421) | copy-start | bytes 1540
  471.6 63.4 %copy-start.12 = (f32[512,128]{0,1:T(8,128)S(1)}, f32[512,128]{0,1:T(8,128)}, u32[]{:S(2)}) copy-start(f32[512,128]{0,1:T(8,128)} %copy-done.11) | copy-start | bytes 786436
  471.6 112.5 %all-reduce.3.cloned.1.call-start = ((), (), s32[]{:S(2)}) async-start(), calls=%async_computation.8 | async-start | bytes 3145728
  533.8 10.3 %slice-start = ((s8[9437184]{0:T(1024)(128)(4,1)}), s8[1048576]{0:T(1024)(128)(4,1)S(1)}, s32[]{:S(2)}) async-start(s8[9437184]{0:T(1024)(128)(4,1)} %bitcast.92), calls=%async_computation.9 | async-start | bytes 2097152
  535.1 9.0 %slice-start.1 = ((s8[9437184]{0:T(1024)(128)(4,1)}), s8[4194304]{0:T(1024)(128)(4,1)S(1)}, s32[]{:S(2)}) async-start(s8[9437184]{0:T(1024)(128)(4,1)} %bitcast.92), calls=%async_computation.10 | async-start | bytes 8388608
  535.1 9.0 %slice-start.2 = ((s8[9437184]{0:T(1024)(128)(4,1)}), s8[4194304]{0:T(1024)(128)(4,1)S(1)}, s32[]{:S(2)}) async-start(s8[9437184]{0:T(1024)(128)(4,1)} %bitcast.92), calls=%async_computation.11 | async-start | bytes 8388608
  535.1 9.0 %copy-start.5 = (f32[4096,128]{0,1:T(8,128)S(1)}, f32[4096,128]{0,1:T(8,128)}, u32[]{:S(2)}) copy-start(f32[4096,128]{0,1:T(8,128)} %copy-done.4) | copy-start | bytes 6291460
  544.2 6.5 %copy-start.10 = (f32[2,512,128]{2,1,0:T(8,128)S(1)}, f32[2,512,128]{2,1,0:T(8,128)}, u32[]{:S(2)}) copy-start(f32[2,512,128]{2,1,0:T(8,128)} %copy-done.9) | copy-start | bytes 1572868
Sparse Core Ops, SparseCore 0:
  10.7 63.6 all-gather.3
  87.9 37.7 reduce-scatter.2
  128.4 55.4 all-gather.5
  411.5 47.6 all-gather.7
  471.8 58.2 reduce-scatter.4
  533.9 50.1 all-reduce.2
where the time goes:
time: 601 us; the launch traced here: 594 us
  waiting for transfers between devices  289 us (48%)
  matrix products  145 us (24%)
  loops' own time  49.5 us (8%)
  other arithmetic  44.7 us (7%)
  local copies, waits for them, and re-layouts  43.3 us (7%)
  between operations  15.5 us (3%)
  starting transfers between devices  7.12 us (1%)
    all_gather x1, waiting for transfers between devices, shards(): lax.all_gather(stacked, TOK, axis=2, tiled=True)  65.2 us
    reduce_scatter x1, waiting for transfers between devices, summed_rows(): running = lax.psum_scatter(running, axis, scatter_dimension=0, tiled=True)  58.4 us
    another operation x1, loops' own time, path_table(): return lax.fori_loop(1, owners, visit_branch, initial)  49.5 us
    all_to_all x1, waiting for transfers between devices, summed_on_arrival(): lax.all_to_all(blocks, axis, split_axis=0, concat_axis=0, tiled=True)  49.5 us
    all_gather x1, waiting for transfers between devices, shards(): every_column = lax.all_gather(own_grads, 'head', axis=2, tiled=True)  47.8 us
    reduce_scatter x1, waiting for transfers between devices, shards(): lax.psum_scatter(partials, 'head', scatter_dimension=2, tiled=True)  35.6 us
    unnamed x7, waiting for transfers between devices  32.8 us
    dot_general x2, matrix products, attend(): grad_prob = jnp.dot(grad_head, value_rows.T, precision=highest)  28.1 us
  transfers between devices with their start and end apart: 7, of which 6 were waited for; matrix products, arithmetic and copies ran while one was open for 12% of the time, Pallas kernels for 0%

commit v1 on v0

v1 whole, which is shorter than its diff:
```python
import functools
import jax, jax.numpy as jnp
from jax import lax
from jax.experimental import pallas as pl
from jax.experimental.pallas import tpu as pltpu
from jax.sharding import Mesh
from jax.sharding import PartitionSpec as P

MESH_ID = pl.DeviceIdType.MESH
RING = 4
OFFSETS = (0, 3, 1, 2)


def turned(axis, by):
    return lax.rem(lax.axis_index(axis) + by, RING)


def greet(axes):
    barrier = pltpu.get_barrier_semaphore()
    for axis in axes:
        for by in (1, 3):
            pl.semaphore_signal(barrier, inc=1, device_id={axis: turned(axis, by)}, device_id_type=MESH_ID)
    pl.semaphore_wait(barrier, 2 * len(axes))


class Wire:
    def __init__(self, send_sem, recv_sem):
        self.send_sem, self.recv_sem, self.sent = send_sem, recv_sem, []

    def copy(self, key, src, dst, axis, by):
        return pltpu.make_async_remote_copy(
            src_ref=src, dst_ref=dst, send_sem=self.send_sem.at[key], recv_sem=self.recv_sem.at[key],
            device_id={axis: turned(axis, by)}, device_id_type=MESH_ID)

    def send(self, key, src, dst, axis, by):
        copy = self.copy(key, src, dst, axis, by)
        copy.start()
        self.sent.append(copy)

    def arrived(self, key, dst, axis, by):
        self.copy(key, dst, dst, axis, by).wait_recv()

    def drain(self):
        for copy in self.sent:
            copy.wait_send()


R0, R1, L0, L1, FR, FL = range(6)


def gather_torus(wire, out, rows):
    quarter = rows // 4
    axes = (("x", "y"), ("y", "x"))

    def slot(half, a, b):
        return a * RING + b if half == 0 else b * RING + a

    def piece(half, a, b, q):
        return out.at[slot(half, a, b), pl.ds((half * 2 + q) * quarter, quarter)]

    def key(half, phase, kind):
        return half * 30 + phase * 6 + kind

    def coords(half, phase, step):
        first, second = axes[half]
        if phase == 0:
            return turned(first, step), lax.axis_index(second)
        return turned(first, OFFSETS[phase - 1]), turned(second, step)

    def ring(half, phase):
        return axes[half][0] if phase == 0 else axes[half][1]

    def send(half, phase, kind, step, q, by):
        part = piece(half, *coords(half, phase, step), q)
        wire.send(key(half, phase, kind), part, part, ring(half, phase), by)

    def arrived(half, phase, kind, step, q):
        part = piece(half, *coords(half, phase, step), q)
        wire.arrived(key(half, phase, kind), part, ring(half, phase), 1)

    def own(phase):
        for kind, q, by in ((R0, 0, 1), (L1, 1, 3), (R1, 1, 1), (L0, 0, 3)):
            for half in (0, 1):
                send(half, phase, kind, 0, q, by)

    def forward(phase):
        for half in (0, 1):
            arrived(half, phase, R0, 3, 0)
            send(half, phase, FR, 3, 0, 1)
            arrived(half, phase, L1, 1, 1)
            send(half, phase, FL, 1, 1, 3)

    def rest(phase):
        for half in (0, 1):
            arrived(half, phase, R1, 3, 1)
            arrived(half, phase, L0, 1, 0)

    def last(phase):
        for half in (0, 1):
            arrived(half, phase, FR, 2, 0)
            arrived(half, phase, FL, 2, 1)

    own(0)
    forward(0)
    own(1)
    rest(0)
    own(2)
    own(3)
    forward(1)
    last(0)
    own(4)
    forward(2)
    forward(3)
    forward(4)
    for phase in (1, 2, 3, 4):
        rest(phase)
        last(phase)


def gather_kernel(rows, own_ref, out_ref, send_sem, recv_sem, local_sem):
    greet(("x", "y"))
    me = lax.axis_index("x") * RING + lax.axis_index("y")
    local = pltpu.make_async_copy(own_ref, out_ref.at[me], local_sem)
    local.start()
    local.wait()
    wire = Wire(send_sem, recv_sem)
    gather_torus(wire, out_ref, rows)
    wire.drain()


def all_gather_plane(own, collective_id):
    rows, cols = own.shape
    return pl.pallas_call(
        functools.partial(gather_kernel, rows),
        out_shape=jax.ShapeDtypeStruct((16, rows, cols), own.dtype),
        in_specs=[pl.BlockSpec(memory_space=pltpu.VMEM)],
        out_specs=pl.BlockSpec(memory_space=pltpu.VMEM),
        scratch_shapes=[pltpu.SemaphoreType.DMA((60,)), pltpu.SemaphoreType.DMA((60,)), pltpu.SemaphoreType.DMA],
        compiler_params=pltpu.CompilerParams(collective_id=collective_id, has_side_effects=True),
    )(own)


S1, S2, S3, T1, T2, T3 = range(6)


def scatter_torus(wire, parts, landing, rows):
    quarter = rows // 4
    axes = (("x", "y"), ("y", "x"))

    def piece(half, a, b, q):
        slot = a * RING + b if half == 0 else b * RING + a
        return parts.at[slot, pl.ds((half * 2 + q) * quarter, quarter)]

    def key(half, phase, kind):
        return half * 30 + phase * 6 + kind

    def ring(half, phase):
        return axes[half][0] if phase == 0 else axes[half][1]

    def part(half, phase, step, q):
        first, second = axes[half]
        if phase == 0:
            return piece(half, turned(first, step), lax.axis_index(second), q)
        return piece(half, turned(first, OFFSETS[phase - 1]), turned(second, step), q)

    def send(half, phase, kind, step, q, by):
        k = key(half, phase, kind)
        wire.send(k, part(half, phase, step, q), landing.at[k], ring(half, phase), by)

    def add(half, phase, kind, step, q):
        k = key(half, phase, kind)
        wire.arrived(k, landing.at[k], ring(half, phase), 1)
        into = part(half, phase, step, q)
        into[...] = into[...] + landing[k]

    def begin(phase):
        for kind, step, q, by in ((S1, 2, 0, 1), (T1, 2, 1, 3), (S2, 1, 1, 1), (T2, 3, 0, 3)):
            for half in (0, 1):
                send(half, phase, kind, step, q, by)

    def relay(phase):
        for half in (0, 1):
            add(half, phase, S1, 1, 0)
            send(half, phase, S3, 1, 0, 1)
            add(half, phase, T1, 3, 1)
            send(half, phase, T3, 3, 1, 3)

    def finish(phase):
        for half in (0, 1):
            add(half, phase, S2, 0, 1)
            add(half, phase, T2, 0, 0)
            add(half, phase, S3, 0, 0)
            add(half, phase, T3, 0, 1)

    begin(4)
    begin(2)
    relay(4)
    begin(3)
    relay(2)
    finish(4)
    begin(1)
    relay(3)
    finish(2)
    relay(1)
    finish(3)
    begin(0)
    relay(0)
    finish(1)
    finish(0)


def scatter_kernel(rows, in_ref, out_ref, parts, landing, send_sem, recv_sem, local_sem):
    greet(("x", "y"))
    me = lax.axis_index("x") * RING + lax.axis_index("y")
    load = pltpu.make_async_copy(in_ref, parts, local_sem)
    load.start()
    load.wait()
    wire = Wire(send_sem, recv_sem)
    scatter_torus(wire, parts, landing, rows)
    wire.drain()
    out_ref[...] = parts[me]


def reduce_scatter_plane(blocks, collective_id):
    _, rows, cols = blocks.shape
    return pl.pallas_call(
        functools.partial(scatter_kernel, rows),
        out_shape=jax.ShapeDtypeStruct((rows, cols), blocks.dtype),
        in_specs=[pl.BlockSpec(memory_space=pl.ANY)],
        out_specs=pl.BlockSpec(memory_space=pltpu.VMEM),
        scratch_shapes=[pltpu.VMEM(blocks.shape, blocks.dtype), pltpu.VMEM((60, rows // 4, cols), blocks.dtype),
                        pltpu.SemaphoreType.DMA((60,)), pltpu.SemaphoreType.DMA((60,)), pltpu.SemaphoreType.DMA],
        compiler_params=pltpu.CompilerParams(collective_id=collective_id, has_side_effects=True),
    )(blocks)


def partner_id():
    return {"core": 1 - lax.axis_index("core")}


def greet_column():
    barrier = pltpu.get_barrier_semaphore()
    for by in (1, 3):
        pl.semaphore_signal(barrier, inc=1, device_id={"z": turned("z", by)}, device_id_type=MESH_ID)
    pl.semaphore_signal(barrier, inc=1, device_id=partner_id(), device_id_type=MESH_ID)
    pl.semaphore_wait(barrier, 3)


def column_gather_kernel(rows, own_ref, out_ref, send_sem, recv_sem, local_sem):
    greet_column()
    core = lax.axis_index("core")
    half = rows // 2

    def piece(step, q, which):
        return out_ref.at[turned("z", step) * 2 + which, pl.ds(q * half, half)]

    local = pltpu.make_async_copy(own_ref, out_ref.at[lax.axis_index("z") * 2 + core], local_sem)
    local.start()
    local.wait()
    wire = Wire(send_sem, recv_sem)

    def over(key, step, q):
        part = piece(step, q, core)
        copy = pltpu.make_async_remote_copy(
            src_ref=part, dst_ref=part, send_sem=send_sem.at[key], recv_sem=recv_sem.at[key],
            device_id=partner_id(), device_id_type=MESH_ID)
        copy.start()
        wire.sent.append(copy)

    def z_send(kind, step, q, by):
        wire.send(kind, piece(step, q, core), piece(step, q, core), "z", by)

    def z_arrived(kind, step, q):
        wire.arrived(kind, piece(step, q, core), "z", 1)
        over(kind + 8, step, q)

    z_send(R0, 0, 0, 1)
    z_send(L1, 0, 1, 3)
    z_send(R1, 0, 1, 1)
    z_send(L0, 0, 0, 3)
    over(6, 0, 0)
    over(7, 0, 1)
    wire.arrived(R0, piece(3, 0, core), "z", 1)
    z_send(FR, 3, 0, 1)
    over(R0 + 8, 3, 0)
    wire.arrived(L1, piece(1, 1, core), "z", 1)
    z_send(FL, 1, 1, 3)
    over(L1 + 8, 1, 1)
    z_arrived(R1, 3, 1)
    z_arrived(L0, 1, 0)
    z_arrived(FR, 2, 0)
    z_arrived(FL, 2, 1)
    other = 1 - core
    for key, step, q in ((6, 0, 0), (7, 0, 1), (R0 + 8, 3, 0), (L1 + 8, 1, 1), (R1 + 8, 3, 1),
                         (L0 + 8, 1, 0), (FR + 8, 2, 0), (FL + 8, 2, 1)):
        wire.arrived(key, piece(step, q, other), "z", 1)
    wire.drain()


def all_gather_column(own, collective_id):
    rows, cols = own.shape
    return pl.pallas_call(
        functools.partial(column_gather_kernel, rows),
        out_shape=jax.ShapeDtypeStruct((8, rows, cols), own.dtype),
        in_specs=[pl.BlockSpec(memory_space=pltpu.VMEM)],
        out_specs=pl.BlockSpec(memory_space=pltpu.VMEM),
        scratch_shapes=[pltpu.SemaphoreType.DMA((14,)), pltpu.SemaphoreType.DMA((14,)), pltpu.SemaphoreType.DMA],
        compiler_params=pltpu.CompilerParams(collective_id=collective_id, has_side_effects=True),
    )(own)


def column_scatter_kernel(rows, in_ref, out_ref, parts, crossed, landing, send_sem, recv_sem, local_sem):
    greet_column()
    core = lax.axis_index("core")
    half = rows // 2
    load = pltpu.make_async_copy(in_ref, parts, local_sem)
    load.start()
    load.wait()
    wire = Wire(send_sem, recv_sem)

    def block(step, which):
        return parts.at[turned("z", step) * 2 + which]

    for i, step in enumerate((2, 1, 3, 0)):
        copy = pltpu.make_async_remote_copy(
            src_ref=block(step, 1 - core), dst_ref=crossed.at[i], send_sem=send_sem.at[6 + i],
            recv_sem=recv_sem.at[6 + i], device_id=partner_id(), device_id_type=MESH_ID)
        copy.start()
        wire.sent.append(copy)

    def cross(i, step):
        wire.arrived(6 + i, crossed.at[i], "z", 1)
        into = block(step, core)
        into[...] = into[...] + crossed[i]

    def part(step, q):
        return parts.at[turned("z", step) * 2 + core, pl.ds(q * half, half)]

    def send(kind, step, q, by):
        wire.send(kind, part(step, q), landing.at[kind], "z", by)

    def add(kind, step, q):
        wire.arrived(kind, landing.at[kind], "z", 1)
        into = part(step, q)
        into[...] = into[...] + landing[kind]

    cross(0, 2)
    send(S1, 2, 0, 1)
    send(T1, 2, 1, 3)
    cross(1, 1)
    send(S2, 1, 1, 1)
    cross(2, 3)
    send(T2, 3, 0, 3)
    add(S1, 1, 0)
    send(S3, 1, 0, 1)
    add(T1, 3, 1)
    send(T3, 3, 1, 3)
    cross(3, 0)
    add(S2, 0, 1)
    add(T2, 0, 0)
    add(S3, 0, 0)
    add(T3, 0, 1)
    wire.drain()
    out_ref[...] = parts[lax.axis_index("z") * 2 + core]


def reduce_scatter_column(blocks, collective_id):
    _, rows, cols = blocks.shape
    return pl.pallas_call(
        functools.partial(column_scatter_kernel, rows),
        out_shape=jax.ShapeDtypeStruct((rows, cols), blocks.dtype),
        in_specs=[pl.BlockSpec(memory_space=pl.ANY)],
        out_specs=pl.BlockSpec(memory_space=pltpu.VMEM),
        scratch_shapes=[pltpu.VMEM(blocks.shape, blocks.dtype), pltpu.VMEM((4, rows, cols), blocks.dtype),
                        pltpu.VMEM((6, rows // 2, cols), blocks.dtype),
                        pltpu.SemaphoreType.DMA((10,)), pltpu.SemaphoreType.DMA((10,)), pltpu.SemaphoreType.DMA],
        compiler_params=pltpu.CompilerParams(collective_id=collective_id, has_side_effects=True),
    )(blocks)


HEAD_DIM = 128
TILE = 128
SPAN = 256
ROWS = 512
BRANCHES = 16
TILE_COUNT = ROWS // TILE
logit_scale = 168.0 ** (-0.5)
HIDDEN_SCORE = -1e30


def split(x, terms):
    parts = []
    for _ in range(terms):
        part = x.astype(jnp.bfloat16)
        parts.append(part)
        x = x - part.astype(jnp.float32)
    return parts


def dot(a, b, contract=((1,), (0,))):
    return lax.dot_general(a, b, (contract, ((), ())), preferred_element_type=jnp.float32)


NT = ((1,), (1,))


def attend_kernel(branch_ref, fork_ref, live_ref, q_ref, g_ref, remote_ref, own_ref,
                  gq_ref, gremote_ref, gown_ref,
                  entry, qcat, gcat, qt, gt, weights, gprob, high, low, delta, gq_acc):
    branch = branch_ref[0]
    live = live_ref[branch]
    for o in range(BRANCHES):
        entry[o] = -1

    def climb(_, b):
        f = fork_ref[jnp.maximum(b - 1, 0)]
        parent = f // TILE_COUNT

        @pl.when(b > 0)
        def _():
            entry[parent] = f % TILE_COUNT

        return jnp.where(b > 0, parent, 0)

    lax.fori_loop(0, BRANCHES - 1, climb, branch)

    both = lambda x: jnp.concatenate([x[:, :HEAD_DIM], x[:, HEAD_DIM:]], axis=0)
    q = both(q_ref[...]) * logit_scale
    q1, q2, q3 = split(q, 3)
    qcat[...] = jnp.concatenate([q1, q1, q2, q2, q1, q3], axis=1)
    qt1, qt2 = split(q.T, 2)
    qt[...] = jnp.concatenate([qt1, qt2], axis=0)
    position = lax.broadcasted_iota(jnp.int32, (2 * ROWS, 1), 0) % ROWS
    g = both(g_ref[...]) * (position < live).astype(jnp.float32)
    g1, g2, g3 = split(g, 3)
    gcat[...] = jnp.concatenate([g1, g1, g2, g2, g1, g3], axis=1)
    gt1, gt2 = split(g.T, 2)
    gt[...] = jnp.concatenate([gt1, gt2], axis=0)
    gremote_ref[...] = jnp.zeros_like(gremote_ref)
    gq_acc[...] = jnp.zeros_like(gq_acc)
    high[...] = jnp.full_like(high, HIDDEN_SCORE)
    low[...] = jnp.zeros_like(low)
    delta[...] = jnp.zeros_like(delta)
    fold = lambda x, op: op(x[:, :HEAD_DIM], x[:, HEAD_DIM:])
    wide = lambda x: jnp.concatenate([x, x], axis=1)

    def remote_key(o):
        return remote_ref[o, :SPAN, :]

    def remote_value(o):
        return remote_ref[o, SPAN:, :]

    def own_key(t):
        return own_ref[t * SPAN : (t + 1) * SPAN, :HEAD_DIM]

    def own_value(t):
        return own_ref[t * SPAN : (t + 1) * SPAN, HEAD_DIM:]

    def over_tiles(visit):
        for t in range(2):
            visit(BRANCHES + t, own_key(t), own_value(t), t)

        def step(o, carry):
            @pl.when(entry[o] >= 0)
            def _():
                visit(o, remote_key(o), remote_value(o), None)

            return carry

        lax.fori_loop(0, BRANCHES, step, 0)

    def score(slot, key, value, own_tile):
        k1, k2, k3 = split(key, 3)
        kcat = jnp.concatenate([k1, k2, k1, k2, k3, k1], axis=1)
        s = dot(qcat[...], kcat, NT)
        column = lax.broadcasted_iota(jnp.int32, (1, SPAN), 1)
        if own_tile is None:
            seen = column // TILE <= entry[slot]
            s = s + jnp.where(seen, 0.0, HIDDEN_SCORE)
        else:
            column = column + own_tile * SPAN
            seen = (column <= position) & (column < live)
            s = jnp.where(seen, s, HIDDEN_SCORE)
        weights[slot] = s
        high[...] = jnp.maximum(high[...], fold(s, jnp.maximum))

    over_tiles(score)
    largest = jnp.max(high[...], axis=1, keepdims=True)
    high[...] = jnp.broadcast_to(largest, high.shape)

    def weigh(slot, key, value, own_tile):
        v1, v2, v3 = split(value, 3)
        gp = dot(gcat[...], jnp.concatenate([v1, v2, v1, v2, v3, v1], axis=1), NT)
        e = jnp.exp(weights[slot] - wide(high[...]))
        weights[slot] = e
        gprob[slot] = gp
        low[...] += fold(e, jnp.add)
        delta[...] += fold(e * gp, jnp.add)

    over_tiles(weigh)
    total = jnp.sum(low[...], axis=1, keepdims=True)
    inverse = 1.0 / total
    low[...] = jnp.broadcast_to(inverse, low.shape)
    delta[...] = jnp.broadcast_to(jnp.sum(delta[...], axis=1, keepdims=True) * inverse, delta.shape)

    def backward(slot, key, value, own_tile):
        p = weights[slot] * wide(low[...])
        ds = p * (gprob[slot] - wide(delta[...]))
        p1, p2 = split(p, 2)
        s1, s2 = split(ds, 2)
        k1, k2 = split(key, 2)
        kk = jnp.concatenate([k1, k2], axis=1)
        gq_acc[...] += dot(s1, kk) + dot(s2, kk)
        gkt = dot(qt[...], s1) + dot(qt[...], s2)
        gvt = dot(gt[...], p1) + dot(gt[...], p2)
        gk = (gkt[:HEAD_DIM] + gkt[HEAD_DIM:]).T
        gv = (gvt[:HEAD_DIM] + gvt[HEAD_DIM:]).T
        if own_tile is None:
            gremote_ref[slot, :SPAN, :] = gk
            gremote_ref[slot, SPAN:, :] = gv
        else:
            gown_ref[own_tile * SPAN : (own_tile + 1) * SPAN, :HEAD_DIM] = gk
            gown_ref[own_tile * SPAN : (own_tile + 1) * SPAN, HEAD_DIM:] = gv

    over_tiles(backward)
    gq = fold(gq_acc[...], jnp.add) * logit_scale
    gq_ref[...] = jnp.concatenate([gq[:ROWS], gq[ROWS:]], axis=1)


def attend(branch, fork_tile, live_len, queries, out_grad, remote, own):
    smem = pl.BlockSpec(memory_space=pltpu.SMEM)
    vmem = pl.BlockSpec(memory_space=pltpu.VMEM)
    f32, bf16 = jnp.float32, jnp.bfloat16
    both = 2 * ROWS
    return pl.pallas_call(
        attend_kernel,
        out_shape=(jax.ShapeDtypeStruct((ROWS, 2 * HEAD_DIM), f32),
                   jax.ShapeDtypeStruct((BRANCHES, 2 * SPAN, HEAD_DIM), f32),
                   jax.ShapeDtypeStruct((ROWS, 2 * HEAD_DIM), f32)),
        in_specs=[smem] * 3 + [vmem] * 4,
        out_specs=[vmem] * 3,
        scratch_shapes=[pltpu.SMEM((BRANCHES,), jnp.int32),
                        pltpu.VMEM((both, 6 * HEAD_DIM), bf16), pltpu.VMEM((both, 6 * HEAD_DIM), bf16),
                        pltpu.VMEM((2 * HEAD_DIM, both), bf16), pltpu.VMEM((2 * HEAD_DIM, both), bf16),
                        pltpu.VMEM((BRANCHES + 2, both, SPAN), f32), pltpu.VMEM((BRANCHES + 2, both, SPAN), f32),
                        pltpu.VMEM((both, HEAD_DIM), f32), pltpu.VMEM((both, HEAD_DIM), f32),
                        pltpu.VMEM((both, HEAD_DIM), f32), pltpu.VMEM((both, 2 * HEAD_DIM), f32)],
        compiler_params=pltpu.CompilerParams(vmem_limit_bytes=64_000_000),
    )(branch, fork_tile, live_len, queries, out_grad, remote, own)


highest = lax.Precision.HIGHEST
HALF = HEAD_DIM // 2


def in_heads(halves):
    return jnp.concatenate(
        [halves[0, :, :HALF], halves[1, :, :HALF], halves[0, :, HALF:], halves[1, :, HALF:]], axis=1
    )


def shards(hidden, queries, out_grad, w_key, w_value, fork_tile, live_len):
    branch = lax.axis_index(("x", "y"))[None].astype(jnp.int32)
    weights = all_gather_plane(jnp.concatenate([w_key, w_value], axis=1), 1)
    partials = jnp.einsum("td,jdc->jtc", hidden, weights, precision=highest)
    own = reduce_scatter_column(partials.reshape(8, 2 * ROWS, HEAD_DIM), 2)
    own = in_heads(own.reshape(2, ROWS, HEAD_DIM))
    fork_rows = jnp.concatenate([own[:SPAN, :HEAD_DIM], own[:SPAN, HEAD_DIM:]], axis=0)
    remote = all_gather_plane(fork_rows, 3)
    grad_query, grad_remote, grad_own = attend(branch, fork_tile, live_len, queries, out_grad, remote, own)
    returned = reduce_scatter_plane(grad_remote, 4)
    grad_own = grad_own.at[:SPAN].add(jnp.concatenate([returned[:SPAN], returned[SPAN:]], axis=1))
    grads = all_gather_column(grad_own, 5)
    blocks = jnp.einsum("htsuc,td->hudsc", grads.reshape(8, ROWS, 2, 2, HALF), hidden, precision=highest)
    summed = reduce_scatter_plane(blocks.reshape(16, hidden.shape[1], HEAD_DIM), 6)
    return (grad_query, grad_own[:, :HEAD_DIM], grad_own[:, HEAD_DIM:], summed[:, :HALF], summed[:, HALF:])


def solution(mesh):
    torus = Mesh(mesh.devices.reshape(4, 4, 4, 2), ("x", "y", "z", "core"))
    tok, head = ("x", "y"), ("z", "core")
    by_both, by_head = P(tok, head), P(head, tok)
    return jax.shard_map(
        shards,
        mesh=torus,
        in_specs=(by_both, by_both, by_both, by_head, by_head, P(), P()),
        out_specs=(by_both, by_both, by_both, by_head, by_head),
        check_vma=False,
    )
```

time: 601 us -> 294 us (0.49)
  waiting for transfers between devices: 289 us -> 0 us
  Pallas kernels: 0 us -> 232 us
  matrix products: 145 us -> 27 us
  loops' own time: 49.5 us -> 0 us
  other arithmetic: 44.7 us -> 2.91 us
  between operations: 15.5 us -> 0.74 us
  local copies, waits for them, and re-layouts: 43.3 us -> 28.9 us
  starting transfers between devices: 7.12 us -> 0 us
    pallas_call x0 -> x7, Pallas kernels: none -> 232 us  [the longest x2 99.8 us: reduce_scatter_plane(): pl.pallas_call(functools.partial(scatter_kernel, rows), out_shape=jax.Sha...]
    dot_general x14 -> x2, matrix products: 145 us -> 27 us  [the longest x1 13.5 us: shards(): partials = jnp.einsum('td,jdc->jtc', hidden, weights, precision=highest)]
    all_gather x3 -> x0, waiting for transfers between devices: 113 us -> none  [the longest x1 65.2 us: shards(): lax.all_gather(stacked, TOK, axis=2, tiled=True)]
    reduce_scatter x2 -> x0, waiting for transfers between devices: 94 us -> none  [the longest x1 58.4 us: summed_rows(): running = lax.psum_scatter(running, axis, scatter_dimension=0, tiled=True)]
    another operation x1 -> x0, loops' own time: 49.5 us -> none  [path_table(): return lax.fori_loop(1, owners, visit_branch, initial)]
    all_to_all x1 -> x0, waiting for transfers between devices: 49.5 us -> none  [summed_on_arrival(): lax.all_to_all(blocks, axis, split_axis=0, concat_axis=0, tiled=True)]
    unnamed x7 -> x0, waiting for transfers between devices: 32.8 us -> none
    another operation x32 -> x0, other arithmetic: 22.4 us -> none
  transfers between devices with their start and end apart: 7 -> 0, of which waited for: 6 -> 0; matrix products, arithmetic and copies ran while one was open for 12% -> 0% of each run, Pallas kernels for 0% -> 0%
where the time goes in v1:
time: 294 us; the launch traced here: 292 us
  Pallas kernels  232 us (79%)
  local copies, waits for them, and re-layouts  28.9 us (10%)
  matrix products  27 us (9%)
    pallas_call x2, Pallas kernels, reduce_scatter_plane(): pl.pallas_call(functools.partial(scatter_kernel, rows), out_shape=jax.Sha...  99.8 us
    pallas_call x2, Pallas kernels, all_gather_plane(): pl.pallas_call(functools.partial(gather_kernel, rows), out_shape=jax.Shap...  68.2 us
    pallas_call x1, Pallas kernels, reduce_scatter_column(): pl.pallas_call(functools.partial(column_scatter_kernel, rows), out_shape=...  27.4 us
    pallas_call x1, Pallas kernels, all_gather_column(): pl.pallas_call(functools.partial(column_gather_kernel, rows), out_shape=j...  26 us
    dot_general x1, matrix products, shards(): partials = jnp.einsum('td,jdc->jtc', hidden, weights, precision=highest)  13.5 us
    dot_general x1, matrix products, shards(): jnp.einsum('htsuc,td->hudsc', grads.reshape(8, ROWS, 2, 2, HALF), hidden,...  13.4 us
    pallas_call x1, Pallas kernels, attend(): pl.pallas_call(attend_kernel, out_shape=(jax.ShapeDtypeStruct((ROWS, 2 *...  10.8 us
    reshape x1, local copies, waits for them, and re-layouts, shards(): blocks.reshape(16, hidden.shape[1], HEAD_DIM)  6.34 us

profile of v1, /device:TPU:0, one launch (start us, length us, event | category | flops | bytes accessed | tf_op | source)
XLA Modules:
  0.0 291.8 jit_solution(1345497018788089275)
XLA Ops:
  0.6 0.0 copy-start
  0.7 1.2 copy.19
  1.9 1.1 copy.20
  3.0 0.9 pad_maximum_fusion.1.own_ref
  3.8 38.6 %shard_map.110 = f32[16,672,128]{2,1,0:T(8,128)} custom-call(f32[672,128]{1,0:T(8,128)} %pad_maximum_fusion.1.own_ref), custom_call_target="tpu_custom_call" | custom-call | tf_op jit(solution)/shard_map/pallas_call | solution.py:133
  42.5 0.0 copy-done
  42.5 13.5 %convolution_bitcast_fusion.1 = f32[16,512,128]{1,2,0:T(8,128)} fusion(f32[16,672,128]{2,1,0:T(8,128)} %shard_map.110, f32[512,672]{0,1:T(8,128)S(1)} %copy-done), kind=kOutput, calls=%fused_computation.1 | convolution fusion | flops 8455716864 | bytes 11075584 | tf_op jit(solution)/shard_map/td,jdc->jtc/dot_general | solution.py:565
  56.0 5.3 %copy.21 = f32[16,512,128]{2,1,0:T(8,128)} copy(f32[16,512,128]{1,2,0:T(8,128)} %convolution_bitcast_fusion.1) | data formatting | bytes 8388608 | tf_op jit(solution)/shard_map/td,jdc->jtc/transpose | solution.py:565
  61.3 27.4 %shard_map.111 = f32[1024,128]{1,0:T(8,128)} custom-call(f32[8,1024,128]{2,1,0:T(8,128)} %bitcast.29), custom_call_target="tpu_custom_call" | custom-call | tf_op jit(solution)/shard_map/pallas_call | solution.py:369
  88.7 1.4 slice_bitcast_fusion.3
  90.1 0.8 fusion.2.own_ref
  91.0 1.1 pad_maximum_fusion.own_ref
  92.1 29.6 %shard_map.112.remote_ref = f32[16,512,128]{2,1,0:T(8,128)} custom-call(f32[512,128]{1,0:T(8,128)} %fusion.2.own_ref), custom_call_target="tpu_custom_call" | custom-call | tf_op jit(solution)/shard_map/pallas_call | solution.py:133
  121.6 10.8 %shard_map.113 = (f32[512,256]{1,0:T(8,128)}, f32[16,512,128]{2,1,0:T(8,128)}, f32[512,256]{1,0:T(8,128)}) custom-call(s32[1]{0:T(128)} %bitcast.branch_ref, s32[15]{0:T(128)} %fork_ref.1, s32[16]{0:T(128)} %live_ref.1, f32[512,256]{1,0:T(8,128)} %q_ref.1, f32[512,256]{1,0:T(8,128)} %g_ref.1, f32[16,512,128]{2,1,0:T(8,128)} %shard_map.112.remote_ref, ...), custom_call_target="tpu_custom_call" | custom-call | tf_op jit(solution)/shard_map/pallas_call | solution.py:535
  132.4 0.0 copy-start.1
  132.4 61.3 %shard_map.114 = f32[512,128]{1,0:T(8,128)} custom-call(f32[16,512,128]{2,1,0:T(8,128)} %get-tuple-element.22.in_ref), custom_call_target="tpu_custom_call" | custom-call | tf_op jit(solution)/shard_map/pallas_call | solution.py:226
  193.7 1.0 fusion.6
  194.7 0.0 copy-done.1
  194.7 0.1 fusion.3.own_ref
  194.8 0.0 copy-start.2
  194.8 0.9 fusion.4
  195.7 0.1 copy-done.2
  195.8 26.0 %shard_map.115 = f32[8,512,256]{2,1,0:T(8,128)} custom-call(f32[512,256]{1,0:T(8,128)} %copy-done.2), custom_call_target="tpu_custom_call" | custom-call | tf_op jit(solution)/shard_map/pallas_call | solution.py:302
  221.8 5.4 %copy.22 = f32[8,512,256]{1,2,0:T(8,128)} copy(f32[8,512,256]{2,1,0:T(8,128)} %shard_map.115) | data formatting | bytes 8388608 | tf_op jit(solution)/shard_map/pallas_call | solution.py:302
  227.2 13.4 %convolution_bitcast_fusion = f32[8,2,672,2,64]{2,4,1,3,0:T(8,128)S(1)} fusion(f32[8,512,2,2,64]{1,4,3,2,0:T(8,128)} %bitcast.28, f32[512,672]{0,1:T(8,128)S(1)} %copy-done), kind=kOutput, calls=%fused_computation | convolution fusion | flops 8455716864 | bytes 11075584 | tf_op jit(solution)/shard_map/htsuc,td->hudsc/dot_general | solution.py:574
  240.7 3.3 %copy.23 = f32[8,2,672,2,64]{2,4,3,1,0:T(8,128)} copy(f32[8,2,672,2,64]{2,4,1,3,0:T(8,128)S(1)} %convolution_bitcast_fusion) | data formatting | bytes 11010048 | tf_op jit(solution)/shard_map/htsuc,td->hudsc/transpose | solution.py:574
  244.0 6.3 %copy.24.in_ref = f32[16,672,128]{2,1,0:T(8,128)} copy(f32[16,672,128]{1,2,0:T(8,128)} %bitcast.27) | data formatting | bytes 11010048 | tf_op jit(solution)/shard_map/reshape | solution.py:575
  250.3 38.5 %shard_map.116 = f32[672,128]{1,0:T(8,128)} custom-call(f32[16,672,128]{2,1,0:T(8,128)} %copy.24.in_ref), custom_call_target="tpu_custom_call" | custom-call | tf_op jit(solution)/shard_map/pallas_call | solution.py:226
  288.9 1.2 fusion.5
  290.1 0.8 copy.26
  291.0 0.8 copy.25
Async XLA Ops:
  0.6 41.9 %copy-start = (f32[512,672]{0,1:T(8,128)S(1)}, f32[512,672]{0,1:T(8,128)}, u32[]{:S(2)}) copy-start(f32[512,672]{0,1:T(8,128)} %param.9) | copy-start | bytes 4128772
  132.4 62.3 %copy-start.1 = (f32[512,256]{1,0:T(8,128)S(1)}, f32[512,256]{1,0:T(8,128)}, u32[]{:S(2)}) copy-start(f32[512,256]{1,0:T(8,128)} %get-tuple-element.21) | copy-start | bytes 1572868
  194.8 1.0 copy-start.2

commit v2 on v0

v2 whole, which is shorter than its diff:
```python
import functools
import jax, jax.numpy as jnp
from jax import lax
from jax.experimental import pallas as pl
from jax.experimental.pallas import tpu as pltpu
from jax.sharding import Mesh
from jax.sharding import PartitionSpec as P

HEAD_DIM = 128
TILE = 128
SPAN = 256
ROWS = 512
BRANCHES = 16
TILE_COUNT = ROWS // TILE
logit_scale = 168.0 ** (-0.5)
HIDDEN_SCORE = -1e30


MESH_ID = pl.DeviceIdType.MESH
RING = 4
OFFSETS = (0, 3, 1, 2)
PLANE = RING * RING
HALF = HEAD_DIM // 2
CHIP_HEADS = 2
AXES = (("x", "y"), ("y", "x"))


def turned(axis, by):
    return lax.rem(lax.axis_index(axis) + by, RING)


def partner_id():
    return {"core": 1 - lax.axis_index("core")}


def greet():
    barrier = pltpu.get_barrier_semaphore()
    for axis in ("x", "y", "z"):
        for by in (1, 3):
            pl.semaphore_signal(barrier, inc=1, device_id={axis: turned(axis, by)}, device_id_type=MESH_ID)
    pl.semaphore_signal(barrier, inc=1, device_id=partner_id(), device_id_type=MESH_ID)
    pl.semaphore_wait(barrier, 7)


class Wire:
    def __init__(self, send_sem, recv_sem):
        self.send_sem, self.recv_sem, self.sent = send_sem, recv_sem, []

    def copy(self, key, src, dst, device):
        return pltpu.make_async_remote_copy(
            src_ref=src, dst_ref=dst, send_sem=self.send_sem.at[key], recv_sem=self.recv_sem.at[key],
            device_id=device, device_id_type=MESH_ID)

    def send(self, key, src, dst, device):
        copy = self.copy(key, src, dst, device)
        copy.start()
        self.sent.append(copy)

    def arrived(self, key, dst):
        self.copy(key, dst, dst, partner_id()).wait_recv()

    def drain(self):
        for copy in self.sent:
            copy.wait_send()


R0, R1, L0, L1, FR, FL = range(6)
S1, S2, S3, T1, T2, T3 = range(6)


class PlanePieces:
    def __init__(self, wire, blocks, rows):
        self.wire, self.blocks, self.quarter = wire, blocks, rows // 4

    def ring(self, half, phase):
        return AXES[half][0] if phase == 0 else AXES[half][1]

    def piece(self, half, phase, step, q):
        first, second = AXES[half]
        if phase == 0:
            a, b = turned(first, step), lax.axis_index(second)
        else:
            a, b = turned(first, OFFSETS[phase - 1]), turned(second, step)
        slot = a * RING + b if half == 0 else b * RING + a
        return self.blocks.at[slot, pl.ds((half * 2 + q) * self.quarter, self.quarter)]

    def key(self, half, phase, kind):
        return half * 30 + phase * 6 + kind


class PlaneGather(PlanePieces):
    def send(self, half, phase, kind, step, q, by):
        part = self.piece(half, phase, step, q)
        axis = self.ring(half, phase)
        self.wire.send(self.key(half, phase, kind), part, part, {axis: turned(axis, by)})

    def arrived(self, half, phase, kind, step, q):
        self.wire.arrived(self.key(half, phase, kind), self.piece(half, phase, step, q))

    def own(self, phase):
        for kind, q, by in ((R0, 0, 1), (L1, 1, 3), (R1, 1, 1), (L0, 0, 3)):
            for half in (0, 1):
                self.send(half, phase, kind, 0, q, by)

    def forward(self, phase):
        for half in (0, 1):
            self.arrived(half, phase, R0, 3, 0)
            self.send(half, phase, FR, 3, 0, 1)
            self.arrived(half, phase, L1, 1, 1)
            self.send(half, phase, FL, 1, 1, 3)

    def rest(self, phase):
        for half in (0, 1):
            self.arrived(half, phase, R1, 3, 1)
            self.arrived(half, phase, L0, 1, 0)

    def last(self, phase):
        for half in (0, 1):
            self.arrived(half, phase, FR, 2, 0)
            self.arrived(half, phase, FL, 2, 1)

    def run(self, between):
        steps = [
            lambda: self.own(0), lambda: self.forward(0), lambda: self.own(1), lambda: self.rest(0),
            lambda: self.own(2), lambda: self.own(3), lambda: self.forward(1), lambda: self.last(0),
            lambda: self.own(4), lambda: self.forward(2),
            lambda: (self.rest(1), self.last(1)), lambda: self.forward(3),
            lambda: (self.rest(2), self.last(2)), lambda: self.forward(4),
            lambda: (self.rest(3), self.last(3)), lambda: (self.rest(4), self.last(4))]
        for number, step in enumerate(steps):
            step()
            for work in between.get(number, ()):
                work()


class PlaneScatter(PlanePieces):
    def __init__(self, wire, blocks, landing, rows):
        super().__init__(wire, blocks, rows)
        self.landing = landing

    def send(self, half, phase, kind, step, q, by):
        k = self.key(half, phase, kind)
        axis = self.ring(half, phase)
        self.wire.send(k, self.piece(half, phase, step, q), self.landing.at[k], {axis: turned(axis, by)})

    def add(self, half, phase, kind, step, q):
        k = self.key(half, phase, kind)
        self.wire.arrived(k, self.landing.at[k])
        into = self.piece(half, phase, step, q)
        into[...] = into[...] + self.landing[k]

    def begin(self, phase):
        for kind, step, q, by in ((S1, 2, 0, 1), (T1, 2, 1, 3), (S2, 1, 1, 1), (T2, 3, 0, 3)):
            for half in (0, 1):
                self.send(half, phase, kind, step, q, by)

    def relay(self, phase):
        for half in (0, 1):
            self.add(half, phase, S1, 1, 0)
            self.send(half, phase, S3, 1, 0, 1)
            self.add(half, phase, T1, 3, 1)
            self.send(half, phase, T3, 3, 1, 3)

    def finish(self, phase):
        for half in (0, 1):
            self.add(half, phase, S2, 0, 1)
            self.add(half, phase, T2, 0, 0)
            self.add(half, phase, S3, 0, 0)
            self.add(half, phase, T3, 0, 1)

    def run(self, between):
        steps = [
            lambda: self.begin(4), lambda: self.begin(2), lambda: self.relay(4), lambda: self.begin(3),
            lambda: self.relay(2), lambda: self.finish(4), lambda: self.begin(1), lambda: self.relay(3),
            lambda: self.finish(2), lambda: self.relay(1), lambda: self.finish(3), lambda: self.begin(0),
            lambda: self.relay(0), lambda: self.finish(1), lambda: self.finish(0)]
        for number, step in enumerate(steps):
            step()
            for work in between.get(number, ()):
                work()


def head_slot(step, which, q):
    return (turned("z", step) * CHIP_HEADS + which) * 2 + q


class ColumnScatter:
    def __init__(self, wire, base, parts, crossed, landing, start, count):
        self.wire, self.base, self.parts = wire, base, parts
        self.crossed, self.landing, self.rows = crossed, landing, pl.ds(start, count)

    def cross_begin(self):
        other = 1 - lax.axis_index("core")
        for i, step in enumerate((2, 1, 3, 0)):
            src = self.parts.at[pl.ds(head_slot(step, other, 0), 2), self.rows]
            self.wire.send(self.base + 6 + i, src, self.crossed.at[i], partner_id())

    def crossed_in(self, i, step):
        self.wire.arrived(self.base + 6 + i, self.crossed.at[i])
        into = self.parts.at[pl.ds(head_slot(step, lax.axis_index("core"), 0), 2), self.rows]
        into[...] = into[...] + self.crossed[i]

    def part(self, step, q):
        return self.parts.at[head_slot(step, lax.axis_index("core"), q), self.rows]

    def send(self, kind, step, q, by):
        self.wire.send(self.base + kind, self.part(step, q), self.landing.at[kind], {"z": turned("z", by)})

    def add(self, kind, step, q):
        self.wire.arrived(self.base + kind, self.landing.at[kind])
        into = self.part(step, q)
        into[...] = into[...] + self.landing[kind]

    def begin(self):
        self.crossed_in(0, 2)
        self.send(S1, 2, 0, 1)
        self.send(T1, 2, 1, 3)
        self.crossed_in(1, 1)
        self.send(S2, 1, 1, 1)
        self.crossed_in(2, 3)
        self.send(T2, 3, 0, 3)

    def relay(self):
        self.add(S1, 1, 0)
        self.send(S3, 1, 0, 1)
        self.add(T1, 3, 1)
        self.send(T3, 3, 1, 3)
        self.crossed_in(3, 0)

    def finish(self):
        self.add(S2, 0, 1)
        self.add(T2, 0, 0)
        self.add(S3, 0, 0)
        self.add(T3, 0, 1)


class ColumnGather:
    def __init__(self, wire, base, grads, start, count):
        self.wire, self.base, self.grads, self.rows = wire, base, grads, pl.ds(start, count)
        self.core = lax.axis_index("core")

    def part(self, step, q, which):
        return self.grads.at[head_slot(step, which, q), self.rows]

    def along(self, kind, step, q, by):
        part = self.part(step, q, self.core)
        self.wire.send(self.base + kind, part, part, {"z": turned("z", by)})

    def across(self, key, step, q):
        part = self.part(step, q, self.core)
        self.wire.send(self.base + key, part, part, partner_id())

    def begin(self):
        self.along(R0, 0, 0, 1)
        self.along(L1, 0, 1, 3)
        self.along(R1, 0, 1, 1)
        self.along(L0, 0, 0, 3)
        self.across(12, 0, 0)
        self.across(13, 0, 1)

    def forward(self):
        self.wire.arrived(self.base + R0, self.part(3, 0, self.core))
        self.along(FR, 3, 0, 1)
        self.across(6 + R0, 3, 0)
        self.wire.arrived(self.base + L1, self.part(1, 1, self.core))
        self.along(FL, 1, 1, 3)
        self.across(6 + L1, 1, 1)

    def near(self):
        for kind, step, q in ((R1, 3, 1), (L0, 1, 0)):
            self.wire.arrived(self.base + kind, self.part(step, q, self.core))
            self.across(6 + kind, step, q)

    def far(self):
        for kind, step, q in ((FR, 2, 0), (FL, 2, 1)):
            self.wire.arrived(self.base + kind, self.part(step, q, self.core))
            self.across(6 + kind, step, q)

    def partner(self, keys):
        for key, step, q in keys:
            self.wire.arrived(self.base + key, self.part(step, q, 1 - self.core))


def split(x, terms):
    parts = []
    for _ in range(terms):
        part = x.astype(jnp.bfloat16)
        parts.append(part)
        x = x - part.astype(jnp.float32)
    return parts


def dot(a, b, contract=((1,), (0,))):
    return lax.dot_general(a, b, (contract, ((), ())), preferred_element_type=jnp.float32)


NT = ((1,), (1,))


def attend_kernel(branch_ref, fork_ref, live_ref, q_ref, g_ref, remote_ref, own_ref,
                  gq_ref, gremote_ref, gown_ref,
                  entry, qcat, gcat, qt, gt, weights, gprob, high, low, delta, gq_acc):
    branch = branch_ref[0]
    live = live_ref[branch]
    for o in range(BRANCHES):
        entry[o] = -1

    def climb(_, b):
        f = fork_ref[jnp.maximum(b - 1, 0)]
        parent = f // TILE_COUNT

        @pl.when(b > 0)
        def _():
            entry[parent] = f % TILE_COUNT

        return jnp.where(b > 0, parent, 0)

    lax.fori_loop(0, BRANCHES - 1, climb, branch)

    both = lambda x: jnp.concatenate([x[:, :HEAD_DIM], x[:, HEAD_DIM:]], axis=0)
    q = both(q_ref[...]) * logit_scale
    q1, q2, q3 = split(q, 3)
    qcat[...] = jnp.concatenate([q1, q1, q2, q2, q1, q3], axis=1)
    qt1, qt2 = split(q.T, 2)
    qt[...] = jnp.concatenate([qt1, qt2], axis=0)
    position = lax.broadcasted_iota(jnp.int32, (2 * ROWS, 1), 0) % ROWS
    g = both(g_ref[...]) * (position < live).astype(jnp.float32)
    g1, g2, g3 = split(g, 3)
    gcat[...] = jnp.concatenate([g1, g1, g2, g2, g1, g3], axis=1)
    gt1, gt2 = split(g.T, 2)
    gt[...] = jnp.concatenate([gt1, gt2], axis=0)
    gremote_ref[...] = jnp.zeros_like(gremote_ref)
    gq_acc[...] = jnp.zeros_like(gq_acc)
    high[...] = jnp.full_like(high, HIDDEN_SCORE)
    low[...] = jnp.zeros_like(low)
    delta[...] = jnp.zeros_like(delta)
    fold = lambda x, op: op(x[:, :HEAD_DIM], x[:, HEAD_DIM:])
    wide = lambda x: jnp.concatenate([x, x], axis=1)

    def remote_key(o):
        return remote_ref[o, :SPAN, :]

    def remote_value(o):
        return remote_ref[o, SPAN:, :]

    def own_key(t):
        return own_ref[t * SPAN : (t + 1) * SPAN, :HEAD_DIM]

    def own_value(t):
        return own_ref[t * SPAN : (t + 1) * SPAN, HEAD_DIM:]

    def over_tiles(visit):
        for t in range(2):
            visit(BRANCHES + t, own_key(t), own_value(t), t)

        def step(o, carry):
            @pl.when(entry[o] >= 0)
            def _():
                visit(o, remote_key(o), remote_value(o), None)

            return carry

        lax.fori_loop(0, BRANCHES, step, 0)

    def score(slot, key, value, own_tile):
        k1, k2, k3 = split(key, 3)
        kcat = jnp.concatenate([k1, k2, k1, k2, k3, k1], axis=1)
        s = dot(qcat[...], kcat, NT)
        column = lax.broadcasted_iota(jnp.int32, (1, SPAN), 1)
        if own_tile is None:
            seen = column // TILE <= entry[slot]
            s = s + jnp.where(seen, 0.0, HIDDEN_SCORE)
        else:
            column = column + own_tile * SPAN
            seen = (column <= position) & (column < live)
            s = jnp.where(seen, s, HIDDEN_SCORE)
        weights[slot] = s
        high[...] = jnp.maximum(high[...], fold(s, jnp.maximum))

    over_tiles(score)
    largest = jnp.max(high[...], axis=1, keepdims=True)
    high[...] = jnp.broadcast_to(largest, high.shape)

    def weigh(slot, key, value, own_tile):
        v1, v2, v3 = split(value, 3)
        gp = dot(gcat[...], jnp.concatenate([v1, v2, v1, v2, v3, v1], axis=1), NT)
        e = jnp.exp(weights[slot] - wide(high[...]))
        weights[slot] = e
        gprob[slot] = gp
        low[...] += fold(e, jnp.add)
        delta[...] += fold(e * gp, jnp.add)

    over_tiles(weigh)
    total = jnp.sum(low[...], axis=1, keepdims=True)
    inverse = 1.0 / total
    low[...] = jnp.broadcast_to(inverse, low.shape)
    delta[...] = jnp.broadcast_to(jnp.sum(delta[...], axis=1, keepdims=True) * inverse, delta.shape)

    def backward(slot, key, value, own_tile):
        p = weights[slot] * wide(low[...])
        ds = p * (gprob[slot] - wide(delta[...]))
        p1, p2 = split(p, 2)
        s1, s2 = split(ds, 2)
        k1, k2 = split(key, 2)
        kk = jnp.concatenate([k1, k2], axis=1)
        gq_acc[...] += dot(s1, kk) + dot(s2, kk)
        gkt = dot(qt[...], s1) + dot(qt[...], s2)
        gvt = dot(gt[...], p1) + dot(gt[...], p2)
        gk = (gkt[:HEAD_DIM] + gkt[HEAD_DIM:]).T
        gv = (gvt[:HEAD_DIM] + gvt[HEAD_DIM:]).T
        if own_tile is None:
            gremote_ref[slot, :SPAN, :] = gk
            gremote_ref[slot, SPAN:, :] = gv
        else:
            gown_ref[own_tile * SPAN : (own_tile + 1) * SPAN, :HEAD_DIM] = gk
            gown_ref[own_tile * SPAN : (own_tile + 1) * SPAN, HEAD_DIM:] = gv

    over_tiles(backward)
    gq = fold(gq_acc[...], jnp.add) * logit_scale
    gq_ref[...] = jnp.concatenate([gq[:ROWS], gq[ROWS:]], axis=1)


def attend(branch, fork_tile, live_len, queries, out_grad, remote, own):
    smem = pl.BlockSpec(memory_space=pltpu.SMEM)
    vmem = pl.BlockSpec(memory_space=pltpu.VMEM)
    f32, bf16 = jnp.float32, jnp.bfloat16
    both = 2 * ROWS
    return pl.pallas_call(
        attend_kernel,
        out_shape=(jax.ShapeDtypeStruct((ROWS, 2 * HEAD_DIM), f32),
                   jax.ShapeDtypeStruct((BRANCHES, 2 * SPAN, HEAD_DIM), f32),
                   jax.ShapeDtypeStruct((ROWS, 2 * HEAD_DIM), f32)),
        in_specs=[smem] * 3 + [vmem] * 4,
        out_specs=[vmem] * 3,
        scratch_shapes=[pltpu.SMEM((BRANCHES,), jnp.int32),
                        pltpu.VMEM((both, 6 * HEAD_DIM), bf16), pltpu.VMEM((both, 6 * HEAD_DIM), bf16),
                        pltpu.VMEM((2 * HEAD_DIM, both), bf16), pltpu.VMEM((2 * HEAD_DIM, both), bf16),
                        pltpu.VMEM((BRANCHES + 2, both, SPAN), f32), pltpu.VMEM((BRANCHES + 2, both, SPAN), f32),
                        pltpu.VMEM((both, HEAD_DIM), f32), pltpu.VMEM((both, HEAD_DIM), f32),
                        pltpu.VMEM((both, HEAD_DIM), f32), pltpu.VMEM((both, 2 * HEAD_DIM), f32)],
        compiler_params=pltpu.CompilerParams(vmem_limit_bytes=64_000_000),
    )(branch, fork_tile, live_len, queries, out_grad, remote, own)


def project_kernel(own_ref, hidden_ref, kv_ref, remote_ref,
                   weights, hidden, left, parts, crossed, landing,
                   plane_send, plane_recv, fork_send, fork_recv, column_send, column_recv, local_sem):
    depth = hidden_ref.shape[1]
    half_depth = depth // 2
    me = lax.axis_index("x") * RING + lax.axis_index("y")
    local = pltpu.make_async_copy(own_ref, weights.at[me], local_sem.at[0])
    local.start()
    rows_in = pltpu.make_async_copy(hidden_ref, hidden, local_sem.at[1])
    rows_in.start()
    greet()
    local.wait()

    def prepare():
        rows_in.wait()
        for half in (0, 1):
            h1, h2, h3 = split(hidden[:, half * half_depth : (half + 1) * half_depth], 3)
            left[half] = jnp.concatenate([h1, h1, h2, h2, h1, h3], axis=1)
        parts[...] = jnp.zeros_like(parts)

    def project(phase, half):
        other = turned(AXES[half][0], OFFSETS[phase - 1])
        slots = [other * RING + i if half == 0 else i * RING + other for i in range(RING)]
        rows = slice(half * half_depth, (half + 1) * half_depth)
        w1, w2, w3 = split(jnp.concatenate([weights[slot, rows, :] for slot in slots], axis=1), 3)
        product = dot(left[half], jnp.concatenate([w1, w2, w1, w2, w3, w1], axis=0))
        for i, slot in enumerate(slots):
            parts[slot] += product[:, i * HEAD_DIM : (i + 1) * HEAD_DIM]

    def both_halves(phase):
        return [functools.partial(project, phase, half) for half in (0, 1)]

    wire = Wire(plane_send, plane_recv)
    PlaneGather(wire, weights, depth).run(
        {0: [prepare], 10: both_halves(1), 12: both_halves(2), 14: both_halves(3), 15: both_halves(4)})

    column = Wire(column_send, column_recv)
    fork, tail = [
        ColumnScatter(column, 10 * i, parts, crossed.at[i], landing.at[i], i * SPAN, SPAN) for i in range(2)]
    fork.cross_begin()
    tail.cross_begin()
    fork.begin()
    fork.relay()
    fork.finish()

    def in_heads(start):
        first, second = [parts[head_slot(0, lax.axis_index("core"), q), start : start + SPAN] for q in range(2)]
        return (jnp.concatenate([first[:, :HALF], second[:, :HALF]], axis=1),
                jnp.concatenate([first[:, HALF:], second[:, HALF:]], axis=1))

    keys, values = in_heads(0)
    remote_ref[me, :SPAN] = keys
    remote_ref[me, SPAN:] = values
    kv_ref[:SPAN] = jnp.concatenate([keys, values], axis=1)
    fork_wire = Wire(fork_send, fork_recv)
    PlaneGather(fork_wire, remote_ref, 2 * SPAN).run(
        {0: [tail.begin], 5: [tail.relay], 9: [tail.finish]})
    keys, values = in_heads(SPAN)
    kv_ref[SPAN:] = jnp.concatenate([keys, values], axis=1)
    for used in (wire, column, fork_wire):
        used.drain()


def project_and_share(own_weights, hidden):
    depth = hidden.shape[1]
    f32, bf16 = jnp.float32, jnp.bfloat16
    dma = pltpu.SemaphoreType.DMA
    return pl.pallas_call(
        project_kernel,
        out_shape=(jax.ShapeDtypeStruct((ROWS, 2 * HEAD_DIM), f32),
                   jax.ShapeDtypeStruct((PLANE, 2 * SPAN, HEAD_DIM), f32)),
        in_specs=[pl.BlockSpec(memory_space=pl.ANY)] * 2,
        out_specs=[pl.BlockSpec(memory_space=pltpu.VMEM)] * 2,
        scratch_shapes=[pltpu.VMEM((PLANE, depth, HEAD_DIM), f32), pltpu.VMEM((ROWS, depth), f32),
                        pltpu.VMEM((2, ROWS, 3 * depth), bf16), pltpu.VMEM((PLANE, ROWS, HEAD_DIM), f32),
                        pltpu.VMEM((2, 4, 2, SPAN, HEAD_DIM), f32), pltpu.VMEM((2, 6, SPAN, HEAD_DIM), f32),
                        dma((60,)), dma((60,)), dma((60,)), dma((60,)), dma((20,)), dma((20,)), dma((2,))],
        compiler_params=pltpu.CompilerParams(
            collective_id=1, has_side_effects=True, vmem_limit_bytes=60_000_000),
    )(own_weights, hidden)


def weight_grad_kernel(remote_ref, own_ref, hidden_ref, key_ref, value_ref, grad_ref,
                       returned, landing, grads, hidden, left, blocks, block_landing,
                       plane_send, plane_recv, block_send, block_recv, column_send, column_recv, local_sem):
    depth = hidden_ref.shape[1]
    me = lax.axis_index("x") * RING + lax.axis_index("y")
    core = lax.axis_index("core")
    load = pltpu.make_async_copy(remote_ref, returned, local_sem.at[0])
    load.start()
    rows_in = pltpu.make_async_copy(hidden_ref, hidden, local_sem.at[1])
    rows_in.start()

    def place(start, keys, values):
        rows = slice(start, start + SPAN)
        for q in range(2):
            part = slice(q * HALF, (q + 1) * HALF)
            grads[head_slot(0, core, q), rows] = jnp.concatenate([keys[:, part], values[:, part]], axis=1)
        key_ref[rows] = keys
        value_ref[rows] = values

    place(SPAN, own_ref[SPAN:, :HEAD_DIM], own_ref[SPAN:, HEAD_DIM:])
    greet()
    load.wait()
    column = Wire(column_send, column_recv)
    fork, tail = [ColumnGather(column, 14 * i, grads, i * SPAN, SPAN) for i in range(2)]

    def prepare():
        rows_in.wait()
        for i in range(2):
            h1, h2, h3 = split(hidden[i * SPAN : (i + 1) * SPAN, :].T, 3)
            left[i] = jnp.concatenate([h1, h1, h2, h2, h1, h3], axis=1)

    def multiply(i, step, which):
        rows = pl.ds(i * SPAN, SPAN)
        slot = head_slot(step, which, 0)
        g1, g2, g3 = split(jnp.concatenate([grads[slot, rows, :], grads[slot + 1, rows, :]], axis=1), 3)
        product = dot(left[i], jnp.concatenate([g1, g2, g1, g2, g3, g1], axis=0))
        for q in range(2):
            new = product[:, q * HEAD_DIM : (q + 1) * HEAD_DIM]
            if i == 0:
                blocks[slot + q] += new
            else:
                blocks[slot + q] = new

    own_keys = ((12, 0, 0), (13, 0, 1))
    near_keys = ((6 + R0, 3, 0), (6 + R1, 3, 1), (6 + L0, 1, 0), (6 + L1, 1, 1))
    far_keys = ((6 + FR, 2, 0), (6 + FL, 2, 1))

    def tail_near():
        tail.near()
        multiply(1, 0, core)
        tail.partner(own_keys)
        multiply(1, 0, 1 - core)
        multiply(1, 3, core)

    def tail_far():
        tail.far()
        multiply(1, 1, core)
        tail.partner(near_keys)
        multiply(1, 3, 1 - core)

    def tail_done():
        multiply(1, 1, 1 - core)
        multiply(1, 2, core)
        tail.partner(far_keys)
        multiply(1, 2, 1 - core)

    plane = Wire(plane_send, plane_recv)
    PlaneScatter(plane, returned, landing, 2 * SPAN).run(
        {0: [tail.begin], 1: [prepare], 2: [tail.forward], 4: [tail_near], 6: [tail_far], 8: [tail_done]})
    place(0, own_ref[:SPAN, :HEAD_DIM] + returned[me, :SPAN], own_ref[:SPAN, HEAD_DIM:] + returned[me, SPAN:])
    fork.begin()
    multiply(0, 0, core)
    fork.forward()
    fork.partner(own_keys)
    multiply(0, 0, 1 - core)
    fork.near()
    multiply(0, 3, core)
    fork.far()
    multiply(0, 1, core)
    fork.partner(near_keys)
    multiply(0, 3, 1 - core)
    multiply(0, 1, 1 - core)
    multiply(0, 2, core)
    fork.partner(far_keys)
    multiply(0, 2, 1 - core)
    block_wire = Wire(block_send, block_recv)
    PlaneScatter(block_wire, blocks, block_landing, depth).run({})
    grad_ref[...] = blocks[me]
    for used in (plane, column, block_wire):
        used.drain()


def weight_grads(grad_remote, grad_own, hidden):
    depth = hidden.shape[1]
    f32, bf16 = jnp.float32, jnp.bfloat16
    dma = pltpu.SemaphoreType.DMA
    anywhere, vmem = pl.BlockSpec(memory_space=pl.ANY), pl.BlockSpec(memory_space=pltpu.VMEM)
    return pl.pallas_call(
        weight_grad_kernel,
        out_shape=(jax.ShapeDtypeStruct((ROWS, HEAD_DIM), f32), jax.ShapeDtypeStruct((ROWS, HEAD_DIM), f32),
                   jax.ShapeDtypeStruct((depth, HEAD_DIM), f32)),
        in_specs=[anywhere, vmem, anywhere],
        out_specs=[vmem] * 3,
        scratch_shapes=[pltpu.VMEM((PLANE, 2 * SPAN, HEAD_DIM), f32), pltpu.VMEM((60, SPAN // 2, HEAD_DIM), f32),
                        pltpu.VMEM((PLANE, ROWS, HEAD_DIM), f32), pltpu.VMEM((ROWS, depth), f32),
                        pltpu.VMEM((2, depth, 6 * SPAN), bf16), pltpu.VMEM((PLANE, depth, HEAD_DIM), f32),
                        pltpu.VMEM((60, depth // 4, HEAD_DIM), f32),
                        dma((60,)), dma((60,)), dma((60,)), dma((60,)), dma((28,)), dma((28,)), dma((2,))],
        compiler_params=pltpu.CompilerParams(
            collective_id=2, has_side_effects=True, vmem_limit_bytes=60_000_000),
    )(grad_remote, grad_own, hidden)


def shards(hidden, queries, out_grad, w_key, w_value, fork_tile, live_len):
    branch = lax.axis_index(("x", "y"))[None].astype(jnp.int32)
    own, remote = project_and_share(jnp.concatenate([w_key, w_value], axis=1), hidden)
    grad_query, grad_remote, grad_own = attend(branch, fork_tile, live_len, queries, out_grad, remote, own)
    grad_key, grad_value, grad_weights = weight_grads(grad_remote, grad_own, hidden)
    return (grad_query, grad_key, grad_value, grad_weights[:, :HALF], grad_weights[:, HALF:])


def solution(mesh):
    torus = Mesh(mesh.devices.reshape(4, 4, 4, 2), ("x", "y", "z", "core"))
    tok, head = ("x", "y"), ("z", "core")
    by_both, by_head = P(tok, head), P(head, tok)
    return jax.shard_map(
        shards,
        mesh=torus,
        in_specs=(by_both, by_both, by_both, by_head, by_head, P(), P()),
        out_specs=(by_both, by_both, by_both, by_head, by_head),
        check_vma=False,
    )
```

time: 601 us -> 218 us (0.36); the launches traced: 594 us -> 217 us
  waiting for transfers between devices: 289 us -> 0 us
  Pallas kernels: 0 us -> 204 us
  matrix products: 145 us -> 0 us
  loops' own time: 49.5 us -> 0 us
  other arithmetic: 44.7 us -> 0.89 us
  local copies, waits for them, and re-layouts: 43.3 us -> 11.5 us
  between operations: 15.5 us -> 0.66 us
  starting transfers between devices: 7.12 us -> 0 us
    pallas_call x0 -> x3, Pallas kernels: none -> 204 us  [the longest x1 108 us: weight_grads(): pl.pallas_call(weight_grad_kernel, out_shape=(jax.ShapeDtypeStruct((ROWS,...]
    dot_general x14 -> x0, matrix products: 145 us -> none  [the longest x2 28.1 us: attend(): grad_prob = jnp.dot(grad_head, value_rows.T, precision=highest)]
    all_gather x3 -> x0, waiting for transfers between devices: 113 us -> none  [the longest x1 65.2 us: shards(): lax.all_gather(stacked, TOK, axis=2, tiled=True)]
    reduce_scatter x2 -> x0, waiting for transfers between devices: 94 us -> none  [the longest x1 58.4 us: summed_rows(): running = lax.psum_scatter(running, axis, scatter_dimension=0, tiled=True)]
    another operation x1 -> x0, loops' own time: 49.5 us -> none  [path_table(): return lax.fori_loop(1, owners, visit_branch, initial)]
    all_to_all x1 -> x0, waiting for transfers between devices: 49.5 us -> none  [summed_on_arrival(): lax.all_to_all(blocks, axis, split_axis=0, concat_axis=0, tiled=True)]
    unnamed x7 -> x0, waiting for transfers between devices: 32.8 us -> none
    another operation x32 -> x0, other arithmetic: 22.4 us -> none
  transfers between devices with their start and end apart: 7 -> 0, of which waited for: 6 -> 0; matrix products, arithmetic and copies ran while one was open for 12% -> 0% of each run, Pallas kernels for 0% -> 0%
where the time goes in v2:
time: 218 us; the launch traced here: 217 us
  Pallas kernels  204 us (94%)
  local copies, waits for them, and re-layouts  11.5 us (5%)
    pallas_call x1, Pallas kernels, weight_grads(): pl.pallas_call(weight_grad_kernel, out_shape=(jax.ShapeDtypeStruct((ROWS,...  108 us
    pallas_call x1, Pallas kernels, project_and_share(): pl.pallas_call(project_kernel, out_shape=(jax.ShapeDtypeStruct((ROWS, 2 *...  85.4 us
    pallas_call x1, Pallas kernels, attend(): pl.pallas_call(attend_kernel, out_shape=(jax.ShapeDtypeStruct((ROWS, 2 *...  10.8 us
    unnamed x7, local copies, waits for them, and re-layouts  10.2 us

profile of v2, /device:TPU:0, one launch (start us, length us, event | category | flops | bytes accessed | tf_op | source)
XLA Modules:
  0.0 217.3 jit_solution(15569305993421070375)
XLA Ops:
  0.6 1.1 copy.12
  1.7 1.1 copy.13
  2.8 0.9 pad_maximum_fusion.own_ref
  3.7 3.0 %copy.14.hidden_ref = f32[512,672]{1,0:T(8,128)} copy(f32[512,672]{0,1:T(8,128)} %param.7) | data formatting | bytes 2752512 | tf_op args[0]
  6.8 85.4 %shard_map.110 = (f32[512,256]{1,0:T(8,128)}, f32[16,512,128]{2,1,0:T(8,128)}) custom-call(f32[672,128]{1,0:T(8,128)} %pad_maximum_fusion.own_ref, f32[512,672]{1,0:T(8,128)} %copy.14.hidden_ref), custom_call_target="tpu_custom_call" | custom-call | tf_op jit(solution)/shard_map/pallas_call | solution.py:512
  92.2 10.8 %shard_map.111 = (f32[512,256]{1,0:T(8,128)}, f32[16,512,128]{2,1,0:T(8,128)}, f32[512,256]{1,0:T(8,128)}) custom-call(s32[1]{0:T(128)} %bitcast.branch_ref, s32[15]{0:T(128)} %fork_ref.1, s32[16]{0:T(128)} %live_ref.1, f32[512,256]{1,0:T(8,128)} %q_ref.1, f32[512,256]{1,0:T(8,128)} %g_ref.1, f32[16,512,128]{2,1,0:T(8,128)} %get-tuple-element.13.remote_ref, ...), custom_call_target="tpu_custom_call" | custom-call | tf_op jit(solution)/shard_map/pallas_call | solution.py:428
  103.0 108.1 %shard_map.112 = (f32[512,128]{1,0:T(8,128)}, f32[512,128]{1,0:T(8,128)}, f32[672,128]{1,0:T(8,128)}) custom-call(f32[16,512,128]{2,1,0:T(8,128)} %get-tuple-element.16.remote_ref, f32[512,256]{1,0:T(8,128)} %get-tuple-element.17.own_ref, f32[512,672]{1,0:T(8,128)} %copy.14.hidden_ref), custom_call_target="tpu_custom_call" | custom-call | tf_op jit(solution)/shard_map/pallas_call | solution.py:624
  211.1 1.2 fusion
  212.3 0.8 copy.17
  213.2 0.8 copy.16
  214.0 1.7 copy.20
  215.7 1.7 copy.21
